TPU v7x, 32 devices: a whole 2x2x4 slice. The times are simulated.
32 devices in a mesh: sec: 2 (over x), el: 16 (over z, y, core).
Axes of the slice: x: 2, y: 2, z: 4, core: 2. Of those that a mesh axis runs over, the one named last changes fastest.
Arguments:
- green_lesser: bfloat16 [2, 256, 64, 2, 128], P('sec', 'el'), may hold values from -6 to 6
- green_greater: bfloat16 [2, 256, 64, 2, 128], P('sec', 'el'), may hold values from -6 to 6
- coulomb: bfloat16 [2, 2, 256, 256], P('sec'), may hold values from -0.375 to 0.375
- pattern: int32 [2, 64], replicated, may hold values from 0 to 511, as said below
Outputs:
- polar: bfloat16 [2, 256, 64, 2, 128], P('sec', 'el')
- screened: bfloat16 [2, 256, 2, 256, 256], P('sec', 'el')
Inputs may be any that keep to these rules, and one draw needn't show every extreme that they name: `pattern`: each row lists 64 distinct tile positions in increasing order.
All inputs are finite; a program needn't handle non-finite values.
Results may differ from a plain program's by a relative error of at most 0.014.
Values may be sent and summed in bfloat16 or wider, within the bound.
A program may use at most 128 MiB of HBM per device.

v0:
```python
import jax
import jax.numpy as jnp
from jax import lax
from jax.sharding import PartitionSpec as P

NB = 256
TR = 8
TC = 16


def with_halo(cells, sides, width):
    for axis, dim in sides:
        count = lax.axis_size(axis)
        ends = count - 1
        head = lax.slice_in_dim(cells, 0, width, axis=dim)
        tail = lax.slice_in_dim(cells, cells.shape[dim] - width, cells.shape[dim], axis=dim)
        cells = jnp.concatenate(
            [
                lax.ppermute(tail, axis, [(i, (i + 1) % count) for i in range(ends)]),
                cells,
                lax.ppermute(head, axis, [((i + 1) % count, i) for i in range(ends)]),
            ],
            axis=dim,
        )
    return cells


def passed_along(array, axis, by):
    length = lax.axis_size(axis)
    pairs = [(i, i + by) for i in range(length) if 0 <= i + by < length]
    return lax.ppermute(array, axis, pairs)


def fourier_tables(length, count):
    rows = lax.broadcasted_iota(jnp.int32, (length, count), 0)
    columns = lax.broadcasted_iota(jnp.int32, (length, count), 1)
    phase = (rows * columns % length).astype(jnp.float32) * (2.0 * jnp.pi / length)
    return (jnp.cos(phase), jnp.sin(phase))


def split_table(table):
    upper_half = table.astype(jnp.bfloat16)
    lower_half = (table - upper_half.astype(jnp.float32)).astype(jnp.bfloat16)
    return (upper_half, lower_half)


def split_product(halves, data):
    first = jnp.dot(halves[0], data, preferred_element_type=jnp.float32)
    return first + jnp.dot(halves[1], data, preferred_element_type=jnp.float32)


def correlate(pieces):
    lesser, greater = pieces
    energies = lesser.shape[0]
    slots = lesser.shape[1]
    width = lesser.shape[3]
    length = 2 * energies
    cosine, sine = fourier_tables(length, energies)
    cosine_halves = split_table(cosine)
    sine_halves = split_table(sine)
    factor = 1.0 / (length * energies**0.5)
    high = lax.Precision.HIGH

    def one_slot(slot_index, result):
        first = lax.dynamic_index_in_dim(lesser, slot_index, 1, keepdims=False)
        second = lax.dynamic_index_in_dim(greater, slot_index, 1, keepdims=False)
        joined = jnp.stack([first, second], axis=1).reshape(energies, 4 * width)
        cos_part = split_product(cosine_halves, joined).reshape(length, 2, 2, width)
        sin_part = split_product(sine_halves, joined).reshape(length, 2, 2, width)
        real_part = cos_part[:, :, 0] + sin_part[:, :, 1]
        imag_part = cos_part[:, :, 1] - sin_part[:, :, 0]
        product_real = real_part[:, 0] * real_part[:, 1] + imag_part[:, 0] * imag_part[:, 1]
        product_imag = imag_part[:, 0] * real_part[:, 1] - real_part[:, 0] * imag_part[:, 1]
        product = jnp.stack([product_real, product_imag], axis=1).reshape(length, 2 * width)
        back_cos = jnp.dot(
            cosine.T, product, precision=high, preferred_element_type=jnp.float32
        ).reshape(energies, 2, width)
        back_sin = jnp.dot(
            sine.T, product, precision=high, preferred_element_type=jnp.float32
        ).reshape(energies, 2, width)
        series_real = back_cos[:, 0] - back_sin[:, 1]
        series_imag = back_cos[:, 1] + back_sin[:, 0]
        value = jnp.stack([-series_imag * factor, series_real * factor], axis=1).astype(
            jnp.bfloat16
        )
        return lax.dynamic_update_index_in_dim(result, value, slot_index, 1)

    start = jnp.zeros(lesser.shape, jnp.bfloat16)
    return lax.fori_loop(0, slots, one_slot, start)


def to_block(tiles):
    count = tiles.shape[0]
    shaped = tiles.reshape(count, NB // TR, NB // TC, 2, TR, TC)
    return shaped.transpose(0, 3, 1, 4, 2, 5).reshape(count, 2, NB, NB)


def make_lookup(listed_row):
    count = listed_row.shape[0]
    total_tiles = NB // TR * (NB // TC)
    positions = jnp.arange(total_tiles, dtype=jnp.int32)
    matches = listed_row[None, :] == positions[:, None]
    ranks = jnp.arange(count, dtype=jnp.int32)
    lookup = jnp.sum(jnp.where(matches, ranks[None, :], 0), axis=1) + jnp.where(
        jnp.any(matches, axis=1), 0, count
    )
    return lookup


def spread_tiles(listed_tiles, lookup):
    blank = jnp.zeros((listed_tiles.shape[0], 1) + listed_tiles.shape[2:], jnp.bfloat16)
    return jnp.take(jnp.concatenate([listed_tiles, blank], axis=1), lookup, axis=1)


def sandwich(matrix, blocks):
    left = jnp.einsum("ij,ecjk->ecik", matrix, blocks, preferred_element_type=jnp.float32).astype(
        jnp.bfloat16
    )
    return jnp.einsum("ecik,lk->ecil", left, matrix, preferred_element_type=jnp.float32)


def sandwich_flipped(matrix, blocks):
    left = jnp.einsum("ji,ecjk->ecik", matrix, blocks, preferred_element_type=jnp.float32).astype(
        jnp.bfloat16
    )
    return jnp.einsum("ecik,kl->ecil", left, matrix, preferred_element_type=jnp.float32)


def on_device(green_lesser, green_greater, coulomb, pattern):
    lesser = green_lesser[0]
    greater = green_greater[0]
    section = lax.axis_index("sec")
    listed_row = lax.dynamic_index_in_dim(pattern, section, 0, keepdims=False)
    lookup = make_lookup(listed_row)
    owned = correlate(
        (
            lax.all_to_all(lesser, "el", split_axis=1, concat_axis=0, tiled=True),
            lax.all_to_all(greater, "el", split_axis=1, concat_axis=0, tiled=True),
        )
    )
    polar = lax.all_to_all(owned, "el", split_axis=0, concat_axis=1, tiled=True)
    tiles = spread_tiles(polar, lookup)
    blocks = to_block(tiles)
    diagonal_term = sandwich(coulomb[0, 0], blocks)
    beside_all = with_halo(blocks[None], (("sec", 0),), 1)
    before_blocks = beside_all[0]
    after_blocks = beside_all[2]
    lower = passed_along(coulomb[0, 1], "sec", 1)
    total = (
        diagonal_term
        + sandwich(coulomb[0, 1], after_blocks)
        + sandwich_flipped(lower, before_blocks)
    )
    return (polar[None], total.astype(jnp.bfloat16)[None])


def solution(mesh):
    in_specs = (
        P("sec", "el", None, None, None),
        P("sec", "el", None, None, None),
        P("sec", None, None, None),
        P(),
    )
    out_specs = (P("sec", "el", None, None, None), P("sec", "el", None, None, None))
    return jax.shard_map(
        on_device, mesh=mesh, in_specs=in_specs, out_specs=out_specs, check_vma=False
    )
```

profile of v0, /device:TPU:0, one launch (start us, length us, event | category | flops | bytes accessed | tf_op | source)
XLA Modules:
  0.0 377.4 jit_solution(642381804469419061)
XLA Ops:
  2.8 7.4 %all-to-all-start = ((bf16[16,64,2,128]{3,2,0,1:T(2,128)(2,1)}), bf16[16,64,2,128]{3,2,0,1:T(2,128)(2,1)S(1)}, u32[]{:S(2)}, u32[]{:S(2)}) async-start(bf16[16,64,2,128]{3,2,0,1:T(2,128)(2,1)} %bitcast.123), calls=%async_computation | async-start | bytes 1048576 | tf_op jit(solution)/shard_map/all_to_all | solution.py:137
  12.5 12.1 %all-to-all-done = bf16[16,64,2,128]{3,2,0,1:T(2,128)(2,1)S(1)} async-done(((bf16[16,64,2,128]{3,2,0,1:T(2,128)(2,1)}), bf16[16,64,2,128]{3,2,0,1:T(2,128)(2,1)S(1)}, u32[]{:S(2)}, u32[]{:S(2)}) %all-to-all-start) | async-done | bytes 524320 | tf_op jit(solution)/shard_map/all_to_all | solution.py:137
  24.5 4.2 %all-to-all-start.1 = ((bf16[16,64,2,128]{3,2,0,1:T(2,128)(2,1)}), bf16[16,64,2,128]{3,2,0,1:T(2,128)(2,1)S(1)}, u32[]{:S(2)}, u32[]{:S(2)}) async-start(bf16[16,64,2,128]{3,2,0,1:T(2,128)(2,1)} %bitcast.122), calls=%async_computation.1 | async-start | bytes 1048576 | tf_op jit(solution)/shard_map/all_to_all | solution.py:138
  29.2 13.8 %all-to-all-done.1 = bf16[16,64,2,128]{3,2,0,1:T(2,128)(2,1)S(1)} async-done(((bf16[16,64,2,128]{3,2,0,1:T(2,128)(2,1)}), bf16[16,64,2,128]{3,2,0,1:T(2,128)(2,1)S(1)}, u32[]{:S(2)}, u32[]{:S(2)}) %all-to-all-start.1) | async-done | bytes 524320 | tf_op jit(solution)/shard_map/all_to_all | solution.py:138
  43.4 65.1 %while.14 = (s32[]{:T(128)}, bf16[256,4,2,128]{3,2,1,0:T(2,128)(2,1)}, bf16[256,4,2,128]{3,2,1,0:T(2,128)(2,1)S(1)}, bf16[256,4,2,128]{3,2,1,0:T(2,128)(2,1)S(1)}, s32[]{:T(128)}) while((s32[]{:T(128)}, bf16[256,4,2,128]{3,2,1,0:T(2,128)(2,1)}, bf16[256,4,2,128]{3,2,1,0:T(2,128)(2,1)S(1)}, bf16[256,4,2,128]{3,2,1,0:T(2,128)(2,1)S(1)}, ...), condition=%wide.region_1.2_spmd.clone, body=%wide.region_0.1_spmd.clone.sunk | while | flops 953581568 | bytes 17695296 | solution.py:89
  46.5 2.4 convolution_add_fusion.5
  48.9 2.4 fusion.141
  51.3 2.4 convolution_add_fusion.4
  62.7 2.4 convolution_add_fusion.5
  65.2 2.4 fusion.141
  67.5 2.4 convolution_add_fusion.4
  79.0 2.4 convolution_add_fusion.5
  81.4 2.4 fusion.141
  83.8 2.4 convolution_add_fusion.4
  95.2 2.4 convolution_add_fusion.5
  97.7 2.4 fusion.141
  100.1 2.4 convolution_add_fusion.4
  108.4 4.2 %all-to-all-start.2 = ((bf16[256,4,2,128]{3,2,1,0:T(2,128)(2,1)}), bf16[256,4,2,128]{3,2,1,0:T(2,128)(2,1)S(1)}, u32[]{:S(2)}, u32[]{:S(2)}) async-start(bf16[256,4,2,128]{3,2,1,0:T(2,128)(2,1)} %get-tuple-element.171), calls=%async_computation.2 | async-start | bytes 1048576 | tf_op jit(solution)/shard_map/all_to_all | solution.py:141
  113.0 13.9 %all-to-all-done.2 = bf16[256,4,2,128]{3,2,1,0:T(2,128)(2,1)S(1)} async-done(((bf16[256,4,2,128]{3,2,1,0:T(2,128)(2,1)}), bf16[256,4,2,128]{3,2,1,0:T(2,128)(2,1)S(1)}, u32[]{:S(2)}, u32[]{:S(2)}) %all-to-all-start.2) | async-done | bytes 524320 | tf_op jit(solution)/shard_map/all_to_all | solution.py:141
  127.1 3.5 gather_fusion
  130.6 5.8 %copy.65 = bf16[16,512,2,128]{3,1,2,0:T(8,128)(2,1)} copy(bf16[16,512,2,128]{3,0,2,1:T(8,128)(2,1)} %bitcast.160) | data formatting | bytes 8388608 | tf_op jit(solution)/shard_map/jit(_take)/gather | solution.py:112
  136.4 33.4 %gather.7 = bf16[16,32,16,2,8,16]{5,4,2,1,3,0:T(8,128)(2,1)} reshape(bf16[16,512,2,128]{3,1,2,0:T(8,128)(2,1)} %copy.65) | data formatting | bytes 8388608 | tf_op jit(solution)/shard_map/jit(_take)/gather | solution.py:112
  169.7 23.0 %select_bitcast_fusion = bf16[16,2,32,8,16,16]{5,3,4,2,1,0:T(8,128)(2,1)} fusion(bf16[16,32,16,2,8,16]{5,4,2,1,3,0:T(8,128)(2,1)} %gather.7, pred[32,16]{1,0:T(8,128)(4,1)S(1)} %compare_and_fusion), kind=kLoop, calls=%fused_computation.75 | loop fusion | flops 2097152 | bytes 8389120 | tf_op jit(solution)/shard_map/transpose | solution.py:95
  192.7 23.0 %copy.66 = bf16[16,2,32,8,16,16]{5,4,3,2,1,0:T(8,128)(2,1)} copy(bf16[16,2,32,8,16,16]{5,3,4,2,1,0:T(8,128)(2,1)} %select_bitcast_fusion) | data formatting | bytes 8388608 | tf_op jit(solution)/shard_map/transpose | solution.py:95
  215.8 39.7 %broadcast_in_dim_reshape.3 = bf16[1,16,2,256,256]{4,3,2,1,0:T(8,128)(2,1)} reshape(bf16[16,2,32,8,16,16]{5,4,3,2,1,0:T(8,128)(2,1)} %copy.66) | data formatting | bytes 8388608 | tf_op jit(solution)/shard_map/broadcast_in_dim;reshape | solution.py:145
  255.5 6.5 %copy.70 = bf16[1,16,2,256,256]{3,4,2,1,0:T(8,128)(2,1)} copy(bf16[1,16,2,256,256]{4,3,2,1,0:T(8,128)(2,1)} %broadcast_in_dim_reshape.3) | data formatting | bytes 8388608 | tf_op jit(solution)/shard_map/broadcast_in_dim;reshape | solution.py:145
  263.3 8.4 %collective-permute-start.1 = (bf16[1,16,2,256,256]{3,4,2,1,0:T(8,128)(2,1)}, bf16[1,16,2,256,256]{3,4,2,1,0:T(8,128)(2,1)}, u32[]{:S(2)}, u32[]{:S(2)}) collective-permute-start(bf16[1,16,2,256,256]{3,4,2,1,0:T(8,128)(2,1)} %copy.70), channel_id=1, source_target_pairs={{0,16},{1,17},{2,18},{3,19},{4,20},{5,21},{6,22},{7,23},{8,24},{9,... | collective-permute-start | bytes 12582920 | tf_op jit(solution)/shard_map/ppermute | solution.py:19
  273.0 39.7 %reshape.129 = bf16[16,2,256,256]{3,2,1,0:T(8,128)(2,1)} reshape(bf16[16,2,32,8,16,16]{5,4,3,2,1,0:T(8,128)(2,1)} %copy.66) | data formatting | bytes 8388608 | tf_op jit(solution)/shard_map/reshape | solution.py:95
  314.0 8.6 %fusion.77 = f32[16,2,256,256]{3,2,1,0:T(8,128)} fusion(bf16[16,2,256,256]{3,2,1,0:T(8,128)(2,1)} %reshape.129, bf16[1,2,256,256]{3,2,1,0:T(8,128)(2,1)S(1)} %copy-done.2), kind=kOutput, calls=%fused_computation.86 | convolution fusion | flops 2149580800 | bytes 12845056 | tf_op jit(solution)/shard_map/ecik,lk->ecil/dot_general | solution.py:119
  322.6 34.2 %collective-permute-done = bf16[1,16,2,256,256]{3,4,2,1,0:T(8,128)(2,1)} collective-permute-done((bf16[1,16,2,256,256]{3,4,2,1,0:T(8,128)(2,1)}, bf16[1,16,2,256,256]{3,4,2,1,0:T(8,128)(2,1)}, u32[]{:S(2)}, u32[]{:S(2)}) %collective-permute-start) | collective-permute-done | bytes 4194336 | tf_op jit(solution)/shard_map/ppermute | solution.py:21
  356.8 8.0 %fusion.73 = f32[16,2,256,256]{3,2,1,0:T(8,128)} fusion(bf16[1,16,2,256,256]{3,4,2,1,0:T(8,128)(2,1)} %collective-permute-done, bf16[1,2,256,256]{3,2,1,0:T(8,128)(2,1)S(1)} %copy-done.2), kind=kOutput, calls=%fused_computation.82 | convolution fusion | flops 2149580800 | bytes 12845056 | tf_op jit(solution)/shard_map/ecik,lk->ecil/dot_general | solution.py:119
  364.8 12.6 %fusion.68 = bf16[1,16,2,256,256]{4,3,2,1,0:T(8,128)(2,1)} fusion(f32[16,2,256,256]{3,2,1,0:T(8,128)} %fusion.77, f32[16,2,256,256]{3,2,1,0:T(8,128)} %fusion.73, bf16[1,16,2,256,256]{3,4,2,1,0:T(8,128)(2,1)} %collective-permute-done.1, bf16[256,256]{1,0:T(8,128)(2,1)S(1)} %collective-permute-done.2), kind=kOutput, calls=%fused_computation.77 | convolution fusion | flops 2155872256 | bytes 25296896 | tf_op jit(solution)/shard_map/ecik,kl->ecil/dot_general | solution.py:126
  (84 shorter events, 45.1 us)
Async XLA Ops:
  0.6 28.1 %copy-start = (s32[2,64]{1,0:T(2,128)S(1)}, s32[2,64]{1,0:T(2,128)}, u32[]{:S(2)}) copy-start(s32[2,64]{1,0:T(2,128)} %param.9) | copy-start | bytes 1540
  2.8 21.7 %all-to-all-start = ((bf16[16,64,2,128]{3,2,0,1:T(2,128)(2,1)}), bf16[16,64,2,128]{3,2,0,1:T(2,128)(2,1)S(1)}, u32[]{:S(2)}, u32[]{:S(2)}) async-start(bf16[16,64,2,128]{3,2,0,1:T(2,128)(2,1)} %bitcast.123), calls=%async_computation | async-start | bytes 1048576 | tf_op jit(solution)/shard_map/all_to_all | solution.py:137
  24.5 18.4 %all-to-all-start.1 = ((bf16[16,64,2,128]{3,2,0,1:T(2,128)(2,1)}), bf16[16,64,2,128]{3,2,0,1:T(2,128)(2,1)S(1)}, u32[]{:S(2)}, u32[]{:S(2)}) async-start(bf16[16,64,2,128]{3,2,0,1:T(2,128)(2,1)} %bitcast.122), calls=%async_computation.1 | async-start | bytes 1048576 | tf_op jit(solution)/shard_map/all_to_all | solution.py:138
  108.4 18.4 %all-to-all-start.2 = ((bf16[256,4,2,128]{3,2,1,0:T(2,128)(2,1)}), bf16[256,4,2,128]{3,2,1,0:T(2,128)(2,1)S(1)}, u32[]{:S(2)}, u32[]{:S(2)}) async-start(bf16[256,4,2,128]{3,2,1,0:T(2,128)(2,1)} %get-tuple-element.171), calls=%async_computation.2 | async-start | bytes 1048576 | tf_op jit(solution)/shard_map/all_to_all | solution.py:141
  255.5 16.2 %copy-start.2 = (bf16[1,2,256,256]{3,2,1,0:T(8,128)(2,1)S(1)}, bf16[1,2,256,256]{3,2,1,0:T(8,128)(2,1)}, u32[]{:S(2)}) copy-start(bf16[1,2,256,256]{3,2,1,0:T(8,128)(2,1)} %param.8) | copy-start | bytes 786436
  262.0 94.8 %collective-permute-start = (bf16[1,16,2,256,256]{3,4,2,1,0:T(8,128)(2,1)}, bf16[1,16,2,256,256]{3,4,2,1,0:T(8,128)(2,1)}, u32[]{:S(2)}, u32[]{:S(2)}) collective-permute-start(bf16[1,16,2,256,256]{3,4,2,1,0:T(8,128)(2,1)} %copy.70), channel_id=1, source_target_pairs={{16,0},{17,1},{18,2},{19,3},{20,4},{21,5},{22,6},{23,7},{24,8},{25... | collective-permute-start | bytes 12582920 | tf_op jit(solution)/shard_map/ppermute | solution.py:21
  263.3 101.6 %collective-permute-start.1 = (bf16[1,16,2,256,256]{3,4,2,1,0:T(8,128)(2,1)}, bf16[1,16,2,256,256]{3,4,2,1,0:T(8,128)(2,1)}, u32[]{:S(2)}, u32[]{:S(2)}) collective-permute-start(bf16[1,16,2,256,256]{3,4,2,1,0:T(8,128)(2,1)} %copy.70), channel_id=1, source_target_pairs={{0,16},{1,17},{2,18},{3,19},{4,20},{5,21},{6,22},{7,23},{8,24},{9,... | collective-permute-start | bytes 12582920 | tf_op jit(solution)/shard_map/ppermute | solution.py:19
  271.7 93.1 %collective-permute-start.2 = (bf16[256,256]{1,0:T(8,128)(2,1)S(1)}, bf16[256,256]{1,0:T(8,128)(2,1)S(1)}, u32[]{:S(2)}, u32[]{:S(2)}) collective-permute-start(bf16[256,256]{1,0:T(8,128)(2,1)S(1)} %slice_bitcast_fusion.2), channel_id=1, source_target_pairs={{0,16},{1,17},{2,18},{3,19},{4,20},{5,21},{6,22},{7,23},{8,24},{9,... | collective-permute-start | bytes 393224 | tf_op jit(solution)/shard_map/ppermute | solution.py:31
  364.8 12.6 %copy-start.1 = (s32[2,64]{1,0:T(2,128)S(1)}, s32[2,64]{1,0:T(2,128)}, u32[]{:S(2)}) copy-start(s32[2,64]{1,0:T(2,128)} %param.9) | copy-start | bytes 1540
where the time goes:
time: 381 us; the launch traced here: 377 us
  local copies, waits for them, and re-layouts  163 us (43%)
  matrix products  86.2 us (23%)
  waiting for transfers between devices  74.1 us (19%)
  starting transfers between devices  26.8 us (7%)
  other arithmetic  26.2 us (7%)
    another operation x2, local copies, waits for them, and re-layouts, on_device(): beside_all = with_halo(blocks[None], (('sec', 0),), 1)  46.2 us
    gather x3, local copies, waits for them, and re-layouts, spread_tiles(): jnp.take(jnp.concatenate([listed_tiles, blank], axis=1), lookup, axis=1)  42.7 us
    reshape x1, local copies, waits for them, and re-layouts, to_block(): return shaped.transpose(0, 3, 1, 4, 2, 5).reshape(count, 2, NB, NB)  39.7 us
    ppermute x1, waiting for transfers between devices, with_halo(): lax.ppermute(head, axis, [((i + 1) % count, i) for i in range(ends)])  34.2 us
    transpose x1, local copies, waits for them, and re-layouts, to_block(): return shaped.transpose(0, 3, 1, 4, 2, 5).reshape(count, 2, NB, NB)  23 us
    transpose x1, other arithmetic, to_block(): return shaped.transpose(0, 3, 1, 4, 2, 5).reshape(count, 2, NB, NB)  23 us
    dot_general x8, matrix products, split_product(): return first + jnp.dot(halves[1], data, preferred_element_type=jnp.float32)  19.5 us
    dot_general x8, matrix products, split_product(): first = jnp.dot(halves[0], data, preferred_element_type=jnp.float32)  19 us
  transfers between devices with their start and end apart: 6, of which 4 were waited for; matrix products, arithmetic and copies ran while one was open for 16% of the time, Pallas kernels for 0%

commit v1 on v0

v1 whole, which is shorter than its diff:
```python
import functools

import jax
import jax.numpy as jnp
import numpy as np
from jax import lax
from jax.experimental import pallas as pl
from jax.experimental.pallas import tpu as pltpu
from jax.sharding import PartitionSpec as P

TR = 8
TC = 16
VMEM_LIMIT = 56 * 1024 * 1024


def halves(table):
    upper = table.astype(jnp.bfloat16)
    lower = (table - upper.astype(np.float32)).astype(jnp.bfloat16)
    return upper, lower


def tables(energies):
    length = 2 * energies
    phase = np.outer(np.arange(length), np.arange(energies)) % length
    phase = phase * (2.0 * np.pi / length)
    cosine = np.cos(phase).astype(np.float32)
    sine = np.sin(phase).astype(np.float32)
    forward = np.concatenate(halves(np.concatenate([cosine, sine], axis=1)), axis=1)
    inverse = np.concatenate(halves(np.concatenate([cosine.T, sine.T], axis=1)), axis=1)
    return jnp.asarray(forward), jnp.asarray(inverse)


def dot32(a, b):
    return jnp.dot(a, b, preferred_element_type=jnp.float32)


def correlate_kernel(factor, x_ref, forward_ref, inverse_ref, out_ref):
    width = x_ref.shape[1] // 4
    x = x_ref[...]
    lesser_r, lesser_i, greater_r, greater_i = (
        x[:, i * width : (i + 1) * width] for i in range(4)
    )
    top = jnp.concatenate([lesser_r, greater_r, lesser_i, greater_i], axis=1)
    bottom = jnp.concatenate([lesser_i, greater_i, -lesser_r, -greater_r], axis=1)
    stacked = jnp.concatenate([top, bottom, top, bottom], axis=0)
    z = dot32(forward_ref[...], stacked)
    lr, gr, li, gi = (z[:, i * width : (i + 1) * width] for i in range(4))
    pr = lr * gr + li * gi
    pi = li * gr - lr * gi
    product = jnp.concatenate(
        [jnp.concatenate([-pi, pr], axis=1), jnp.concatenate([-pr, -pi], axis=1)], axis=0
    )
    high = product.astype(jnp.bfloat16)
    low = (product - high.astype(jnp.float32)).astype(jnp.bfloat16)
    depth = product.shape[0]
    series = dot32(inverse_ref[...], jnp.concatenate([high, high], axis=0))
    series = series + dot32(inverse_ref[:, :depth], low)
    out_ref[...] = (series * factor).astype(jnp.bfloat16)


def correlate(x, slots):
    energies, columns = x.shape
    width = columns // slots
    forward, inverse = tables(energies)
    factor = 1.0 / (2 * energies * energies**0.5)
    return pl.pallas_call(
        functools.partial(correlate_kernel, factor),
        grid=(slots,),
        in_specs=[
            pl.BlockSpec((energies, width), lambda s: (0, s)),
            pl.BlockSpec(forward.shape, lambda s: (0, 0)),
            pl.BlockSpec(inverse.shape, lambda s: (0, 0)),
        ],
        out_specs=pl.BlockSpec((energies, width // 2), lambda s: (0, s)),
        out_shape=jax.ShapeDtypeStruct((energies, columns // 2), jnp.bfloat16),
        compiler_params=pltpu.CompilerParams(vmem_limit_bytes=VMEM_LIMIT),
    )(x, forward, inverse)


def screen_kernel(count, terms, batch, *refs):
    tile_refs = refs[:terms]
    matrix_ref, row_ref, col_ref, spread_ref, out_ref, picked_ref, mask_ref = refs[terms:]
    nb = matrix_ref.shape[1]

    @pl.when(pl.program_id(0) == 0)
    def _():
        for t in range(terms):
            depth = row_ref.shape[2]
            position = lax.broadcasted_iota(jnp.int32, (nb, depth), 0)
            chosen = jnp.where(position == row_ref[t], 1.0, 0.0).astype(jnp.bfloat16)
            picked_ref[t] = dot32(matrix_ref[t], chosen).astype(jnp.bfloat16)
            lane = lax.broadcasted_iota(jnp.int32, (count, nb), 1) // TC
            mask_ref[t] = jnp.where(lane == col_ref[t], 1.0, 0.0)

    left = [[[] for _ in range(2)] for _ in range(batch)]
    for t in range(terms):
        width = spread_ref.shape[0]
        rows = jnp.concatenate(
            [tile_refs[t][b, :, c * width : (c + 1) * width] for b in range(batch) for c in range(2)],
            axis=0,
        )
        wide = dot32(rows, spread_ref[...])
        mask = mask_ref[t]
        for b in range(batch):
            for c in range(2):
                start = (2 * b + c) * count
                pieces = [
                    (wide[start : start + count, r * nb : (r + 1) * nb] * mask).astype(jnp.bfloat16)
                    for r in range(TR)
                ]
                stacked = jnp.concatenate(pieces, axis=0)
                left[b][c].append(dot32(picked_ref[t], stacked).astype(jnp.bfloat16))
    right = jnp.concatenate([matrix_ref[t] for t in range(terms)], axis=1)
    for b in range(batch):
        for c in range(2):
            joined = jnp.concatenate(left[b][c], axis=1)
            total = lax.dot_general(
                joined, right, (((1,), (1,)), ((), ())), preferred_element_type=jnp.float32
            )
            out_ref[b, c] = total.astype(jnp.bfloat16)


def screen(tiles, matrices, listed):
    terms = len(tiles)
    energies, count, both = tiles[0].shape
    nb = matrices.shape[1]
    batch = 2 if energies % 2 == 0 else 1
    width = both // 2
    tile_row = listed // (nb // TC)
    tile_col = listed % (nb // TC)
    offsets = jnp.arange(TR, dtype=jnp.int32)
    row_index = (tile_row[:, None, :] * TR + offsets[None, :, None]).reshape(terms, 1, TR * count)
    col_index = tile_col[:, :, None]
    entry = np.arange(width)[:, None]
    column = np.arange(TR * nb)[None, :]
    spread = jnp.asarray(
        (entry == column // nb * TC + column % TC).astype(np.float32).astype(jnp.bfloat16)
    )
    whole = lambda shape: pl.BlockSpec(shape, lambda i: (0,) * len(shape))
    return pl.pallas_call(
        functools.partial(screen_kernel, count, terms, batch),
        grid=(energies // batch,),
        in_specs=[pl.BlockSpec((batch, count, both), lambda i: (i, 0, 0))] * terms
        + [whole(matrices.shape), whole(row_index.shape), whole(col_index.shape), whole(spread.shape)],
        out_specs=pl.BlockSpec((batch, 2, nb, nb), lambda i: (i, 0, 0, 0)),
        out_shape=jax.ShapeDtypeStruct((energies, 2, nb, nb), jnp.bfloat16),
        scratch_shapes=[
            pltpu.VMEM((terms, nb, TR * count), jnp.bfloat16),
            pltpu.VMEM((terms, count, nb), jnp.float32),
        ],
        compiler_params=pltpu.CompilerParams(vmem_limit_bytes=VMEM_LIMIT),
    )(*tiles, matrices, row_index, col_index, spread)


def on_device(sections, owners, green_lesser, green_greater, coulomb, pattern):
    _, local, count, _, width = green_lesser.shape
    slots = count // owners
    energies = local * owners
    section = lax.axis_index("sec")

    both = jnp.stack([green_lesser[0], green_greater[0]], axis=2)
    both = both.reshape(local, owners, slots * 4 * width).transpose(1, 0, 2)
    gathered = lax.all_to_all(both, "el", split_axis=0, concat_axis=0, tiled=True)
    owned = correlate(gathered.reshape(energies, slots * 4 * width), slots)
    back = lax.all_to_all(
        owned.reshape(owners, local, slots * 2 * width), "el", split_axis=0, concat_axis=0, tiled=True
    )
    polar = back.transpose(1, 0, 2).reshape(local, count, 2 * width)

    tiles = [polar]
    matrices = [coulomb[0, 0]]
    listed = [lax.dynamic_index_in_dim(pattern, section, 0, keepdims=False)]
    if sections == 2:
        swap = [(0, 1), (1, 0)]
        tiles.append(lax.ppermute(polar, "sec", swap))
        other = lax.ppermute(coulomb[0, 1], "sec", swap)
        matrices.append(jnp.where(section == 0, coulomb[0, 1], other.T))
        listed.append(lax.dynamic_index_in_dim(pattern, 1 - section, 0, keepdims=False))
    elif sections > 2:
        up = [(i, i + 1) for i in range(sections - 1)]
        down = [(i + 1, i) for i in range(sections - 1)]
        tiles.append(lax.ppermute(polar, "sec", up))
        tiles.append(lax.ppermute(polar, "sec", down))
        matrices.append(lax.ppermute(coulomb[0, 1], "sec", up).T)
        matrices.append(coulomb[0, 1])
        before = jnp.maximum(section - 1, 0)
        after = jnp.minimum(section + 1, sections - 1)
        listed.append(lax.dynamic_index_in_dim(pattern, before, 0, keepdims=False))
        listed.append(lax.dynamic_index_in_dim(pattern, after, 0, keepdims=False))
    screened = screen(tiles, jnp.stack(matrices), jnp.stack(listed))
    return polar.reshape(1, local, count, 2, width), screened[None]


def solution(mesh):
    in_specs = (
        P("sec", "el", None, None, None),
        P("sec", "el", None, None, None),
        P("sec", None, None, None),
        P(),
    )
    out_specs = (P("sec", "el", None, None, None), P("sec", "el", None, None, None))
    return jax.shard_map(
        functools.partial(on_device, mesh.shape["sec"], mesh.shape["el"]),
        mesh=mesh,
        in_specs=in_specs,
        out_specs=out_specs,
        check_vma=False,
    )
```

time: 381 us -> 98 us (0.26)
  local copies, waits for them, and re-layouts: 163 us -> 5.22 us
  matrix products: 86.2 us -> 0 us
  waiting for transfers between devices: 74.1 us -> 21.5 us
  blocking collectives: 0 us -> 32 us
  Pallas kernels: 0 us -> 25.2 us
  other arithmetic: 26.2 us -> 4.78 us
  starting transfers between devices: 26.8 us -> 8.14 us
    dot_general x27 -> x0, matrix products: 86.2 us -> none  [the longest x8 19.5 us: split_product(): return first + jnp.dot(halves[1], data, preferred_element_type=jnp.float32)]
    another operation x2 -> x5, local copies, waits for them, and re-layouts: 46.2 us -> 2.15 us  [the longest x1 1.16 us: on_device(): return (polar.reshape(1, local, count, 2, width), screened[None])]
    gather x3 -> x0, local copies, waits for them, and re-layouts: 42.7 us -> none  [spread_tiles(): jnp.take(jnp.concatenate([listed_tiles, blank], axis=1), lookup, axis=1)]
    reshape x5 -> x2, local copies, waits for them, and re-layouts: 40.1 us -> 1.14 us  [the longest x1 0.82 us: on_device(): both = both.reshape(local, owners, slots * 4 * width).transpose(1, 0, 2)]
    all_to_all x0 -> x1, blocking collectives: none -> 32 us  [on_device(): lax.all_to_all(both, 'el', split_axis=0, concat_axis=0, tiled=True)]
    all_to_all x3 -> x1, waiting for transfers between devices: 39.8 us -> 12.4 us  [on_device(): lax.all_to_all(owned.reshape(owners, local, slots * 2 * width), 'el', spl...]
    pallas_call x0 -> x2, Pallas kernels: none -> 25.2 us  [the longest x1 15 us: screen(): pl.pallas_call(functools.partial(screen_kernel, count, terms, batch), gri...]
    ppermute x3 -> x2, waiting for transfers between devices: 34.2 us -> 9.13 us  [the longest x1 9.13 us: on_device(): tiles.append(lax.ppermute(polar, 'sec', swap))]
  transfers between devices with their start and end apart: 6 -> 3, of which waited for: 4 -> 2; matrix products, arithmetic and copies ran while one was open for 16% -> 4% of each run, Pallas kernels for 0% -> 0%
where the time goes in v1:
time: 98 us; the launch traced here: 97.6 us
  blocking collectives  32 us (33%)
  Pallas kernels  25.2 us (26%)
  waiting for transfers between devices  21.5 us (22%)
  starting transfers between devices  8.14 us (8%)
  local copies, waits for them, and re-layouts  5.22 us (5%)
  other arithmetic  4.78 us (5%)
    all_to_all x1, blocking collectives, on_device(): lax.all_to_all(both, 'el', split_axis=0, concat_axis=0, tiled=True)  32 us
    pallas_call x1, Pallas kernels, screen(): pl.pallas_call(functools.partial(screen_kernel, count, terms, batch), gri...  15 us
    all_to_all x1, waiting for transfers between devices, on_device(): lax.all_to_all(owned.reshape(owners, local, slots * 2 * width), 'el', spl...  12.4 us
    pallas_call x1, Pallas kernels, correlate(): pl.pallas_call(functools.partial(correlate_kernel, factor), grid=(slots,)...  10.2 us
    ppermute x1, waiting for transfers between devices, on_device(): tiles.append(lax.ppermute(polar, 'sec', swap))  9.13 us
    all_to_all x1, starting transfers between devices, on_device(): lax.all_to_all(owned.reshape(owners, local, slots * 2 * width), 'el', spl...  5.02 us
    another operation x1, other arithmetic, on_device(): both = jnp.stack([green_lesser[0], green_greater[0]], axis=2)  2.77 us
  transfers between devices with their start and end apart: 3, of which 2 were waited for; matrix products, arithmetic and copies ran while one was open for 4% of the time, Pallas kernels for 0%

profile of v1, /device:TPU:0, one launch (start us, length us, event | category | flops | bytes accessed | tf_op | source)
XLA Modules:
  0.0 97.6 jit_solution(14675587338453831248)
XLA Ops:
  0.6 2.8 %pad_maximum_fusion = bf16[16,64,2,2,128]{4,3,1,0,2:T(2,128)(2,1)S(1)} fusion(bf16[16,64,1,2,128]{4,3,1,0,2:T(2,128)(2,1)} %bitcast.25, bf16[16,64,1,2,128]{4,3,1,0,2:T(2,128)(2,1)} %bitcast.26), kind=kLoop, calls=%fused_computation | loop fusion | flops 524288 | bytes 2097152 | tf_op jit(solution)/shard_map/stack | solution.py:161
  3.4 0.8 copy.46
  4.2 0.8 reshape.225
  5.0 0.0 copy-start.1
  5.0 0.6 copy.47
  5.6 0.0 copy-start.3
  5.6 32.0 %all_to_all.10 = bf16[16,16,2048]{2,1,0:T(8,128)(2,1)} all-to-all(bf16[16,16,2048]{2,1,0:T(8,128)(2,1)S(1)} %copy.47), channel_id=1, replica_groups=mesh['sec'=2,'el'=16] {'el'}, dimensions={0} | all-to-all | bytes 2097152 | tf_op jit(solution)/shard_map/all_to_all | solution.py:163
  37.6 10.2 %shard_map.86 = bf16[256,1024]{1,0:T(8,128)(2,1)} custom-call(bf16[256,2048]{1,0:T(8,128)(2,1)} %bitcast.20, bf16[512,1024]{1,0:T(8,128)(2,1)} %constant.53.clone.forward_ref, bf16[256,2048]{1,0:T(8,128)(2,1)} %constant.54.clone.inverse_ref), custom_call_target="tpu_custom_call" | custom-call | tf_op jit(solution)/shard_map/pallas_call | solution.py:66
  47.9 5.0 %all-to-all-start.1 = ((bf16[16,16,1024]{2,1,0:T(8,128)(2,1)}), bf16[16,16,1024]{2,1,0:T(8,128)(2,1)S(1)}, u32[]{:S(2)}, u32[]{:S(2)}) async-start(bf16[16,16,1024]{2,1,0:T(8,128)(2,1)} %bitcast.23), calls=%async_computation.1 | async-start | bytes 1048576 | tf_op jit(solution)/shard_map/all_to_all | solution.py:165
  52.9 0.0 copy-done.1
  52.9 0.1 copy.54
  53.0 1.6 %collective-permute-start.1 = (bf16[256,256]{0,1:T(8,128)(2,1)S(1)}, bf16[256,256]{0,1:T(8,128)(2,1)S(1)}, u32[]{:S(2)}, u32[]{:S(2)}) collective-permute-start(bf16[256,256]{0,1:T(8,128)(2,1)S(1)} %bitcast.27), channel_id=1, source_target_pairs={{0,16},{16,0},{1,17},{17,1},{2,18},{18,2},{3,19},{19,3},{4,20},{20... | collective-permute-start | bytes 393224 | tf_op jit(solution)/shard_map/ppermute | solution.py:176
  54.6 0.1 add.57
  54.7 0.0 copy-done.3
  54.7 0.1 add.55
  54.8 12.4 %all-to-all-done.1 = bf16[16,16,1024]{2,1,0:T(8,128)(2,1)S(1)} async-done(((bf16[16,16,1024]{2,1,0:T(8,128)(2,1)}), bf16[16,16,1024]{2,1,0:T(8,128)(2,1)S(1)}, u32[]{:S(2)}, u32[]{:S(2)}) %all-to-all-start.1) | async-done | bytes 524320 | tf_op jit(solution)/shard_map/all_to_all | solution.py:165
  67.2 0.3 copy.48
  67.5 0.3 reshape.228.refs_0_
  67.8 0.0 copy-start
  67.8 1.6 %collective-permute-start = (bf16[16,64,256]{2,1,0:T(8,128)(2,1)S(1)}, bf16[16,64,256]{2,1,0:T(8,128)(2,1)S(1)}, u32[]{:S(2)}, u32[]{:S(2)}) collective-permute-start(bf16[16,64,256]{2,1,0:T(8,128)(2,1)S(1)} %reshape.228.refs_0_), channel_id=1, source_target_pairs={{0,16},{16,0},{1,17},{17,1},{2,18},{18,2},{3,19},{19,3},{4,20},{20... | collective-permute-start | bytes 1572872 | tf_op jit(solution)/shard_map/ppermute | solution.py:175
  69.3 0.6 broadcast_add_fusion.refs_3_
  69.9 0.1 copy.53
  70.0 0.1 copy.52
  70.1 0.6 add_select_fusion.refs_4_
  70.8 0.0 collective-permute-done.1
  70.8 0.7 pad_maximum_fusion.1.refs_2_
  71.5 1.2 %reshape_reshape.3 = bf16[1,16,64,2,128]{4,3,2,1,0:T(2,128)(2,1)} reshape(bf16[16,16,1024]{2,1,0:T(8,128)(2,1)S(1)} %copy.48) | data formatting | bytes 1048576 | tf_op jit(solution)/shard_map/reshape;reshape | solution.py:191
  72.7 9.1 %collective-permute-done.refs_1_ = bf16[16,64,256]{2,1,0:T(8,128)(2,1)S(1)} collective-permute-done((bf16[16,64,256]{2,1,0:T(8,128)(2,1)S(1)}, bf16[16,64,256]{2,1,0:T(8,128)(2,1)S(1)}, u32[]{:S(2)}, u32[]{:S(2)}) %collective-permute-start) | collective-permute-done | bytes 524320 | tf_op jit(solution)/shard_map/ppermute | solution.py:175
  81.8 0.0 copy-done
  81.8 0.0 copy-start.2
  81.8 0.8 copy-done.2
  82.6 15.0 %shard_map.87 = bf16[16,2,256,256]{3,2,1,0:T(8,128)(2,1)} custom-call(bf16[16,64,256]{2,1,0:T(8,128)(2,1)} %copy-done, bf16[16,64,256]{2,1,0:T(8,128)(2,1)} %copy-done.2, bf16[2,256,256]{2,1,0:T(8,128)(2,1)} %pad_maximum_fusion.1.refs_2_, s32[2,1,512]{2,1,0:T(1,128)} %broadcast_add_fusion.refs_3_, s32[2,64,1]{2,1,0:T(8,128)} %add_select_fusion.refs_4_, ...), custom_call_target="tpu_custom_call" | custom-call | tf_op jit(solution)/shard_map/pallas_call | solution.py:140
  (6 shorter events, 0.1 us)
Async XLA Ops:
  5.0 47.9 %copy-start.1 = (bf16[1,2,256,256]{3,2,1,0:T(8,128)(2,1)S(1)}, bf16[1,2,256,256]{3,2,1,0:T(8,128)(2,1)}, u32[]{:S(2)}) copy-start(bf16[1,2,256,256]{3,2,1,0:T(8,128)(2,1)} %param.9) | copy-start | bytes 786436
  5.6 49.1 %copy-start.3 = (s32[2,64]{1,0:T(2,128)S(1)}, s32[2,64]{1,0:T(2,128)}, u32[]{:S(2)}) copy-start(s32[2,64]{1,0:T(2,128)} %param.10) | copy-start | bytes 1540
  47.9 19.3 %all-to-all-start.1 = ((bf16[16,16,1024]{2,1,0:T(8,128)(2,1)}), bf16[16,16,1024]{2,1,0:T(8,128)(2,1)S(1)}, u32[]{:S(2)}, u32[]{:S(2)}) async-start(bf16[16,16,1024]{2,1,0:T(8,128)(2,1)} %bitcast.23), calls=%async_computation.1 | async-start | bytes 1048576 | tf_op jit(solution)/shard_map/all_to_all | solution.py:165
  53.0 17.8 %collective-permute-start.1 = (bf16[256,256]{0,1:T(8,128)(2,1)S(1)}, bf16[256,256]{0,1:T(8,128)(2,1)S(1)}, u32[]{:S(2)}, u32[]{:S(2)}) collective-permute-start(bf16[256,256]{0,1:T(8,128)(2,1)S(1)} %bitcast.27), channel_id=1, source_target_pairs={{0,16},{16,0},{1,17},{17,1},{2,18},{18,2},{3,19},{19,3},{4,20},{20... | collective-permute-start | bytes 393224 | tf_op jit(solution)/shard_map/ppermute | solution.py:176
  67.8 14.1 %copy-start = (bf16[16,64,256]{2,1,0:T(8,128)(2,1)}, bf16[16,64,256]{2,1,0:T(8,128)(2,1)S(1)}, u32[]{:S(2)}) copy-start(bf16[16,64,256]{2,1,0:T(8,128)(2,1)S(1)} %reshape.228.refs_0_) | copy-start | bytes 1572868
  67.8 14.0 %collective-permute-start = (bf16[16,64,256]{2,1,0:T(8,128)(2,1)S(1)}, bf16[16,64,256]{2,1,0:T(8,128)(2,1)S(1)}, u32[]{:S(2)}, u32[]{:S(2)}) collective-permute-start(bf16[16,64,256]{2,1,0:T(8,128)(2,1)S(1)} %reshape.228.refs_0_), channel_id=1, source_target_pairs={{0,16},{16,0},{1,17},{17,1},{2,18},{18,2},{3,19},{19,3},{4,20},{20... | collective-permute-start | bytes 1572872 | tf_op jit(solution)/shard_map/ppermute | solution.py:175
  81.8 0.8 copy-start.2

commit v2 on v1

--- a/solution.py
+++ b/solution.py
@@ -25,56 +25,226 @@
     phase = phase * (2.0 * np.pi / length)
     cosine = np.cos(phase).astype(np.float32)
     sine = np.sin(phase).astype(np.float32)
-    forward = np.concatenate(halves(np.concatenate([cosine, sine], axis=1)), axis=1)
-    inverse = np.concatenate(halves(np.concatenate([cosine.T, sine.T], axis=1)), axis=1)
-    return jnp.asarray(forward), jnp.asarray(inverse)
+    real = np.stack([cosine, sine], axis=2).reshape(length, length)
+    imag = np.stack([-sine, cosine], axis=2).reshape(length, length)
+    forward = np.concatenate(halves(np.concatenate([real, imag], axis=0)), axis=1)
+    out_r = np.concatenate([-sine.T, -cosine.T], axis=1)
+    out_i = np.concatenate([cosine.T, -sine.T], axis=1)
+    inverse = np.stack([out_r, out_i], axis=1).reshape(length, 2 * length)
+    return jnp.asarray(forward), jnp.asarray(np.concatenate(halves(inverse), axis=1))
 
 
 def dot32(a, b):
     return jnp.dot(a, b, preferred_element_type=jnp.float32)
 
 
-def correlate_kernel(factor, x_ref, forward_ref, inverse_ref, out_ref):
-    width = x_ref.shape[1] // 4
-    x = x_ref[...]
-    lesser_r, lesser_i, greater_r, greater_i = (
-        x[:, i * width : (i + 1) * width] for i in range(4)
-    )
-    top = jnp.concatenate([lesser_r, greater_r, lesser_i, greater_i], axis=1)
-    bottom = jnp.concatenate([lesser_i, greater_i, -lesser_r, -greater_r], axis=1)
-    stacked = jnp.concatenate([top, bottom, top, bottom], axis=0)
-    z = dot32(forward_ref[...], stacked)
-    lr, gr, li, gi = (z[:, i * width : (i + 1) * width] for i in range(4))
-    pr = lr * gr + li * gi
-    pi = li * gr - lr * gi
-    product = jnp.concatenate(
-        [jnp.concatenate([-pi, pr], axis=1), jnp.concatenate([-pr, -pi], axis=1)], axis=0
-    )
+def correlate_slot(factor, lesser, greater, forward_ref, inverse_ref):
+    energies, _, width = lesser.shape
+    length = 2 * energies
+    joined = jnp.concatenate(
+        [lesser.reshape(length, width), greater.reshape(length, width)], axis=1
+    )
+    z = dot32(forward_ref[:, :length], joined) + dot32(forward_ref[:, length:], joined)
+    lr, gr = z[:length, :width], z[:length, width:]
+    li, gi = z[length:, :width], z[length:, width:]
+    product = jnp.concatenate([lr * gr + li * gi, li * gr - lr * gi], axis=0)
     high = product.astype(jnp.bfloat16)
     low = (product - high.astype(jnp.float32)).astype(jnp.bfloat16)
-    depth = product.shape[0]
-    series = dot32(inverse_ref[...], jnp.concatenate([high, high], axis=0))
-    series = series + dot32(inverse_ref[:, :depth], low)
-    out_ref[...] = (series * factor).astype(jnp.bfloat16)
-
-
-def correlate(x, slots):
-    energies, columns = x.shape
-    width = columns // slots
+    depth = 2 * length
+    first = dot32(inverse_ref[:, :depth], jnp.concatenate([high, low], axis=1))
+    series = first[:, :width] + first[:, width:] + dot32(inverse_ref[:, depth:], high)
+    return (series * factor).astype(jnp.bfloat16).reshape(energies, 2, width)
+
+
+def exchange_kernel(
+    owners,
+    sections,
+    factor,
+    lesser_ref,
+    greater_ref,
+    coupling_ref,
+    forward_hbm,
+    inverse_hbm,
+    *refs,
+):
+    sides = 1 if sections == 2 else 2
+    polar_ref = refs[0]
+    beside_refs = refs[1 : 1 + sides]
+    other_ref = refs[1 + sides]
+    (
+        x_ref,
+        d_ref,
+        forward_ref,
+        inverse_ref,
+        table_sem,
+        in_send,
+        in_recv,
+        out_send,
+        out_recv,
+        side_send,
+        side_recv,
+        c_send,
+        c_recv,
+    ) = refs[2 + sides :]
+    slots = x_ref.shape[0]
+    local = polar_ref.shape[0]
+    me = lax.axis_index("el")
+    section = lax.axis_index("sec")
+    mesh_id = pl.DeviceIdType.MESH
+    if sections == 2:
+        targets = [1 - section]
+    else:
+        targets = [
+            lax.rem(section + 1, sections),
+            lax.rem(section + sections - 1, sections),
+        ]
+
+    load_f = pltpu.make_async_copy(forward_hbm, forward_ref, table_sem.at[0])
+    load_i = pltpu.make_async_copy(inverse_hbm, inverse_ref, table_sem.at[1])
+    load_f.start()
+    load_i.start()
+
+    barrier = pltpu.get_barrier_semaphore()
+
+    def greet(step, carry):
+        peer = lax.rem(me + step, owners)
+        pl.semaphore_signal(barrier, inc=1, device_id={"el": peer}, device_id_type=mesh_id)
+        return carry
+
+    lax.fori_loop(1, owners, greet, 0)
+    for target in targets:
+        pl.semaphore_signal(barrier, inc=1, device_id={"sec": target}, device_id_type=mesh_id)
+    pl.semaphore_wait(barrier, owners - 1 + sides)
+
+    mine = pl.ds(me * local, local)
+    for slot in range(slots):
+        for which, source in enumerate((lesser_ref, greater_ref)):
+
+            def send(step, carry, slot=slot, which=which, source=source):
+                peer = lax.rem(me + step, owners)
+                pltpu.make_async_remote_copy(
+                    src_ref=source.at[:, peer, slot],
+                    dst_ref=x_ref.at[slot, which, mine],
+                    send_sem=in_send.at[slot],
+                    recv_sem=in_recv.at[slot],
+                    device_id={"el": peer},
+                    device_id_type=mesh_id,
+                ).start()
+                return carry
+
+            pltpu.make_async_copy(
+                source.at[:, me, slot], x_ref.at[slot, which, mine], in_recv.at[slot]
+            ).start()
+            lax.fori_loop(1, owners, send, 0)
+
+    shared = pltpu.make_async_remote_copy(
+        src_ref=coupling_ref,
+        dst_ref=other_ref,
+        send_sem=c_send,
+        recv_sem=c_recv,
+        device_id={"sec": targets[0]},
+        device_id_type=mesh_id,
+    )
+    shared.start()
+    load_f.wait()
+    load_i.wait()
+
+    def arrive(slot):
+        whole = polar_ref.at[:, :, slot]
+        pltpu.make_async_copy(whole, whole, out_recv.at[slot]).wait()
+
+    def forward_copy(slot, side):
+        return pltpu.make_async_remote_copy(
+            src_ref=polar_ref.at[:, :, slot],
+            dst_ref=beside_refs[side].at[:, :, slot],
+            send_sem=side_send.at[side, slot],
+            recv_sem=side_recv.at[side, slot],
+            device_id={"sec": targets[side]},
+            device_id_type=mesh_id,
+        )
+
+    def pass_on(slot):
+        arrive(slot)
+        for side in range(sides):
+            forward_copy(slot, side).start()
+
+    for slot in range(slots):
+        whole = x_ref.at[slot]
+        pltpu.make_async_copy(whole, whole, in_recv.at[slot]).wait()
+        d_ref[slot] = correlate_slot(
+            factor, x_ref[slot, 0], x_ref[slot, 1], forward_ref, inverse_ref
+        )
+        pltpu.make_async_copy(
+            d_ref.at[slot, mine], polar_ref.at[:, me, slot], out_recv.at[slot]
+        ).start()
+
+        def give(step, carry, slot=slot):
+            peer = lax.rem(me + step, owners)
+            pltpu.make_async_remote_copy(
+                src_ref=d_ref.at[slot, pl.ds(peer * local, local)],
+                dst_ref=polar_ref.at[:, me, slot],
+                send_sem=out_send.at[slot],
+                recv_sem=out_recv.at[slot],
+                device_id={"el": peer},
+                device_id_type=mesh_id,
+            ).start()
+            return carry
+
+        lax.fori_loop(1, owners, give, 0)
+        if slot >= 2:
+            pass_on(slot - 2)
+    for slot in range(max(slots - 2, 0), slots):
+        pass_on(slot)
+
+    sent = (owners - 1) * local
+    for slot in range(slots):
+        part = x_ref.at[slot, :, pl.ds(0, sent)]
+        pltpu.make_async_copy(part, part, in_send.at[slot]).wait()
+        part = d_ref.at[slot, pl.ds(0, sent)]
+        pltpu.make_async_copy(part, part, out_send.at[slot]).wait()
+        for side in range(sides):
+            forward_copy(slot, side).wait()
+    shared.wait()
+
+
+def exchange(owners, sections, lesser, greater, coupling):
+    local, count, _, width = lesser.shape
+    slots = count // owners
+    energies = local * owners
+    sides = 1 if sections == 2 else 2
     forward, inverse = tables(energies)
-    factor = 1.0 / (2 * energies * energies**0.5)
+    split = (local, owners, slots, 2, width)
+    tile_shape = jax.ShapeDtypeStruct(split, jnp.bfloat16)
+    anywhere = pl.BlockSpec(memory_space=pl.ANY)
+    near = pl.BlockSpec(memory_space=pltpu.VMEM)
+    dma = pltpu.SemaphoreType.DMA
     return pl.pallas_call(
-        functools.partial(correlate_kernel, factor),
-        grid=(slots,),
-        in_specs=[
-            pl.BlockSpec((energies, width), lambda s: (0, s)),
-            pl.BlockSpec(forward.shape, lambda s: (0, 0)),
-            pl.BlockSpec(inverse.shape, lambda s: (0, 0)),
+        functools.partial(
+            exchange_kernel, owners, sections, 1.0 / (2 * energies * energies**0.5)
+        ),
+        in_specs=[anywhere] * 5,
+        out_specs=[near] * (2 + sides),
+        out_shape=[tile_shape] * (1 + sides)
+        + [jax.ShapeDtypeStruct(coupling.shape, coupling.dtype)],
+        scratch_shapes=[
+            pltpu.VMEM((slots, 2, energies, 2, width), jnp.bfloat16),
+            pltpu.VMEM((slots, energies, 2, width), jnp.bfloat16),
+            pltpu.VMEM(forward.shape, jnp.bfloat16),
+            pltpu.VMEM(inverse.shape, jnp.bfloat16),
+            dma((2,)),
+            dma((slots,)),
+            dma((slots,)),
+            dma((slots,)),
+            dma((slots,)),
+            dma((sides, slots)),
+            dma((sides, slots)),
+            dma(()),
+            dma(()),
         ],
-        out_specs=pl.BlockSpec((energies, width // 2), lambda s: (0, s)),
-        out_shape=jax.ShapeDtypeStruct((energies, columns // 2), jnp.bfloat16),
-        compiler_params=pltpu.CompilerParams(vmem_limit_bytes=VMEM_LIMIT),
-    )(x, forward, inverse)
+        compiler_params=pltpu.CompilerParams(
+            collective_id=0, has_side_effects=True, vmem_limit_bytes=VMEM_LIMIT
+        ),
+    )(lesser.reshape(split), greater.reshape(split), coupling, forward, inverse)
 
 
 def screen_kernel(count, terms, batch, *refs):
@@ -154,40 +324,26 @@
 
 def on_device(sections, owners, green_lesser, green_greater, coulomb, pattern):
     _, local, count, _, width = green_lesser.shape
-    slots = count // owners
-    energies = local * owners
     section = lax.axis_index("sec")
-
-    both = jnp.stack([green_lesser[0], green_greater[0]], axis=2)
-    both = both.reshape(local, owners, slots * 4 * width).transpose(1, 0, 2)
-    gathered = lax.all_to_all(both, "el", split_axis=0, concat_axis=0, tiled=True)
-    owned = correlate(gathered.reshape(energies, slots * 4 * width), slots)
-    back = lax.all_to_all(
-        owned.reshape(owners, local, slots * 2 * width), "el", split_axis=0, concat_axis=0, tiled=True
-    )
-    polar = back.transpose(1, 0, 2).reshape(local, count, 2 * width)
-
-    tiles = [polar]
+    polar, *beside, other = exchange(
+        owners, sections, green_lesser[0], green_greater[0], coulomb[0, 1]
+    )
+    flat = lambda t: t.reshape(local, count, 2 * width)
     matrices = [coulomb[0, 0]]
     listed = [lax.dynamic_index_in_dim(pattern, section, 0, keepdims=False)]
     if sections == 2:
-        swap = [(0, 1), (1, 0)]
-        tiles.append(lax.ppermute(polar, "sec", swap))
-        other = lax.ppermute(coulomb[0, 1], "sec", swap)
         matrices.append(jnp.where(section == 0, coulomb[0, 1], other.T))
         listed.append(lax.dynamic_index_in_dim(pattern, 1 - section, 0, keepdims=False))
-    elif sections > 2:
-        up = [(i, i + 1) for i in range(sections - 1)]
-        down = [(i + 1, i) for i in range(sections - 1)]
-        tiles.append(lax.ppermute(polar, "sec", up))
-        tiles.append(lax.ppermute(polar, "sec", down))
-        matrices.append(lax.ppermute(coulomb[0, 1], "sec", up).T)
-        matrices.append(coulomb[0, 1])
-        before = jnp.maximum(section - 1, 0)
-        after = jnp.minimum(section + 1, sections - 1)
+    else:
+        before = lax.rem(section + sections - 1, sections)
+        after = lax.rem(section + 1, sections)
+        matrices.append(jnp.where(section > 0, other.T, 0))
+        matrices.append(jnp.where(section < sections - 1, coulomb[0, 1], 0))
         listed.append(lax.dynamic_index_in_dim(pattern, before, 0, keepdims=False))
         listed.append(lax.dynamic_index_in_dim(pattern, after, 0, keepdims=False))
-    screened = screen(tiles, jnp.stack(matrices), jnp.stack(listed))
+    screened = screen(
+        [flat(t) for t in (polar, *beside)], jnp.stack(matrices), jnp.stack(listed)
+    )
     return polar.reshape(1, local, count, 2, width), screened[None]
 
 

time: 98 us -> 76.1 us (0.78)
  Pallas kernels: 25.2 us -> 65.2 us
  blocking collectives: 32 us -> 0 us
  waiting for transfers between devices: 21.5 us -> 0 us
  starting transfers between devices: 8.14 us -> 0 us
  other arithmetic: 4.78 us -> 2 us
  local copies, waits for them, and re-layouts: 5.22 us -> 7.91 us
    pallas_call x1, Pallas kernels: 10.2 us -> 50.2 us  [exchange(): pl.pallas_call(functools.partial(exchange_kernel, owners, sections, 1.0 /...]
    all_to_all x1 -> x0, blocking collectives: 32 us -> none  [on_device(): lax.all_to_all(both, 'el', split_axis=0, concat_axis=0, tiled=True)]
    all_to_all x1 -> x0, waiting for transfers between devices: 12.4 us -> none  [on_device(): lax.all_to_all(owned.reshape(owners, local, slots * 2 * width), 'el', spl...]
    ppermute x2 -> x0, waiting for transfers between devices: 9.13 us -> none  [the longest x1 9.13 us: on_device(): tiles.append(lax.ppermute(polar, 'sec', swap))]
    all_to_all x1 -> x0, starting transfers between devices: 5.02 us -> none  [on_device(): lax.all_to_all(owned.reshape(owners, local, slots * 2 * width), 'el', spl...]
    ppermute x2 -> x0, starting transfers between devices: 3.12 us -> none  [the longest x1 1.56 us: on_device(): other = lax.ppermute(coulomb[0, 1], 'sec', swap)]
    another operation x3 -> x2, other arithmetic: 3.52 us -> 0.74 us  [on_device(): jnp.stack(matrices)]
    reshape x2, local copies, waits for them, and re-layouts: 1.14 us -> 3.35 us  [on_device(): flat = lambda t: t.reshape(local, count, 2 * width)]
  transfers between devices with their start and end apart: 3 -> 0, of which waited for: 2 -> 0; matrix products, arithmetic and copies ran while one was open for 4% -> 0% of each run, Pallas kernels for 0% -> 0%
where the time goes in v2:
time: 76.1 us; the launch traced here: 75.8 us
  Pallas kernels  65.2 us (86%)
  local copies, waits for them, and re-layouts  7.91 us (10%)
  other arithmetic  2 us (3%)
    pallas_call x1, Pallas kernels, exchange(): pl.pallas_call(functools.partial(exchange_kernel, owners, sections, 1.0 /...  50.2 us
    pallas_call x1, Pallas kernels, screen(): pl.pallas_call(functools.partial(screen_kernel, count, terms, batch), gri...  15 us
    reshape x2, local copies, waits for them, and re-layouts, on_device(): flat = lambda t: t.reshape(local, count, 2 * width)  3.35 us
    another operation x1, local copies, waits for them, and re-layouts, on_device(): jnp.stack(matrices)  1.64 us

profile of v2, /device:TPU:0, one launch (start us, length us, event | category | flops | bytes accessed | tf_op | source)
XLA Modules:
  0.0 75.8 jit_solution(9012735265291268927)
XLA Ops:
  0.6 0.8 %constant_dynamic-slice_fusion.1 = (s32[1,64]{1,0:T(1,128)S(1)}, s32[1,64]{1,0:T(1,128)S(1)}) fusion(s32[2,64]{1,0:T(2,128)} %param.10, s32[]{:T(128)S(6)} %select_n.40, s32[]{:T(128)S(6)} %select_n.41), kind=kLoop, calls=%fused_computation.17 | loop fusion | bytes 1032 | tf_op jit(solution)/shard_map/jit(dynamic_index_in_dim)/dynamic_slice | solution.py:333
  1.4 0.1 add.57
  1.5 0.1 add.55
  1.6 0.6 broadcast_add_fusion.refs_3_
  2.2 0.1 copy.22
  2.3 0.1 copy.21
  2.4 0.7 add_select_fusion.refs_4_
  3.0 1.6 %slice_bitcast_fusion = (bf16[1,256,256]{2,1,0:T(8,128)(2,1)S(1)}, bf16[256,256]{1,0:T(8,128)(2,1)}) fusion(bf16[1,2,256,256]{3,2,1,0:T(8,128)(2,1)} %param.9), kind=kLoop, calls=%fused_computation.3 | loop fusion | bytes 524288 | tf_op jit(solution)/shard_map/stack;squeeze | solution.py:345
  4.7 0.0 copy-start.1
  4.7 50.2 %shard_map.86 = (bf16[16,16,4,2,128]{4,3,2,1,0:T(2,128)(2,1)}, bf16[16,16,4,2,128]{4,3,2,1,0:T(2,128)(2,1)}, bf16[256,256]{1,0:T(8,128)(2,1)}) custom-call(bf16[16,16,4,2,128]{4,3,2,1,0:T(2,128)(2,1)} %bitcast.20, bf16[16,16,4,2,128]{4,3,2,1,0:T(2,128)(2,1)} %bitcast.21, bf16[256,256]{1,0:T(8,128)(2,1)} %get-tuple-element.9.coupling_ref, ...), custom_call_target="tpu_custom_call" | custom-call | tf_op jit(solution)/shard_map/pallas_call | solution.py:221
  54.9 0.0 copy-start
  54.9 2.2 %reshape.224.refs_1_ = bf16[16,64,256]{2,1,0:T(8,128)(2,1)} reshape(bf16[16,16,4,2,128]{4,3,2,1,0:T(2,128)(2,1)} %get-tuple-element.6) | data formatting | bytes 1048576 | tf_op jit(solution)/shard_map/reshape | solution.py:331
  57.2 1.0 %copy.20 = bf16[256,256]{0,1:T(8,128)(2,1)S(1)} copy(bf16[256,256]{1,0:T(8,128)(2,1)} %get-tuple-element.7) | data formatting | bytes 262144 | tf_op jit(solution)/shard_map/pallas_call | solution.py:221
  58.2 0.0 copy-done.1
  58.2 0.7 pad_maximum_fusion.refs_2_
  58.9 0.0 copy-done
  58.9 1.1 %reshape.223.refs_0_ = bf16[16,64,256]{2,1,0:T(8,128)(2,1)} reshape(bf16[16,16,4,2,128]{4,3,2,1,0:T(2,128)(2,1)S(1)} %copy-done) | data formatting | bytes 1048576 | tf_op jit(solution)/shard_map/reshape | solution.py:331
  60.0 15.0 %shard_map.87 = bf16[16,2,256,256]{3,2,1,0:T(8,128)(2,1)} custom-call(bf16[16,64,256]{2,1,0:T(8,128)(2,1)} %reshape.223.refs_0_, bf16[16,64,256]{2,1,0:T(8,128)(2,1)} %reshape.224.refs_1_, bf16[2,256,256]{2,1,0:T(8,128)(2,1)} %pad_maximum_fusion.refs_2_, s32[2,1,512]{2,1,0:T(1,128)} %broadcast_add_fusion.refs_3_, s32[2,64,1]{2,1,0:T(8,128)} %add_select_fusion.refs_4_, ...), custom_call_target="tpu_custom_call" | custom-call | tf_op jit(solution)/shard_map/pallas_call | solution.py:310
  75.1 0.8 %copy.24 = bf16[1,16,64,2,128]{4,3,2,1,0:T(2,128)(2,1)} copy(bf16[1,16,64,2,128]{4,3,2,1,0:T(2,128)(2,1)S(1)} %bitcast.19) | data formatting | bytes 1048576
  (4 shorter events, 0.0 us)
Async XLA Ops:
  4.7 53.5 %copy-start.1 = (bf16[1,2,256,256]{3,2,1,0:T(8,128)(2,1)S(1)}, bf16[1,2,256,256]{3,2,1,0:T(8,128)(2,1)}, u32[]{:S(2)}) copy-start(bf16[1,2,256,256]{3,2,1,0:T(8,128)(2,1)} %param.9) | copy-start | bytes 786436
  54.9 4.0 %copy-start = (bf16[16,16,4,2,128]{4,3,2,1,0:T(2,128)(2,1)S(1)}, bf16[16,16,4,2,128]{4,3,2,1,0:T(2,128)(2,1)}, u32[]{:S(2)}) copy-start(bf16[16,16,4,2,128]{4,3,2,1,0:T(2,128)(2,1)} %get-tuple-element.5) | copy-start | bytes 1572868

commit v3 on v2

--- a/solution.py
+++ b/solution.py
@@ -62,7 +62,7 @@
     factor,
     lesser_ref,
     greater_ref,
-    coupling_ref,
+    coulomb_ref,
     forward_hbm,
     inverse_hbm,
     *refs,
@@ -116,12 +116,16 @@
         pl.semaphore_signal(barrier, inc=1, device_id={"sec": target}, device_id_type=mesh_id)
     pl.semaphore_wait(barrier, owners - 1 + sides)
 
+    def peer_at(turn):
+        away = (turn + 1) // 2 * (2 * (turn % 2) - 1)
+        return lax.rem(me + owners // 2 + away, owners)
+
     mine = pl.ds(me * local, local)
     for slot in range(slots):
         for which, source in enumerate((lesser_ref, greater_ref)):
 
-            def send(step, carry, slot=slot, which=which, source=source):
-                peer = lax.rem(me + step, owners)
+            def send(turn, carry, slot=slot, which=which, source=source):
+                peer = peer_at(turn)
                 pltpu.make_async_remote_copy(
                     src_ref=source.at[:, peer, slot],
                     dst_ref=x_ref.at[slot, which, mine],
@@ -135,10 +139,10 @@
             pltpu.make_async_copy(
                 source.at[:, me, slot], x_ref.at[slot, which, mine], in_recv.at[slot]
             ).start()
-            lax.fori_loop(1, owners, send, 0)
+            lax.fori_loop(0, owners - 1, send, 0)
 
     shared = pltpu.make_async_remote_copy(
-        src_ref=coupling_ref,
+        src_ref=coulomb_ref.at[1],
         dst_ref=other_ref,
         send_sem=c_send,
         recv_sem=c_recv,
@@ -178,8 +182,8 @@
             d_ref.at[slot, mine], polar_ref.at[:, me, slot], out_recv.at[slot]
         ).start()
 
-        def give(step, carry, slot=slot):
-            peer = lax.rem(me + step, owners)
+        def give(turn, carry, slot=slot):
+            peer = peer_at(turn)
             pltpu.make_async_remote_copy(
                 src_ref=d_ref.at[slot, pl.ds(peer * local, local)],
                 dst_ref=polar_ref.at[:, me, slot],
@@ -190,7 +194,7 @@
             ).start()
             return carry
 
-        lax.fori_loop(1, owners, give, 0)
+        lax.fori_loop(0, owners - 1, give, 0)
         if slot >= 2:
             pass_on(slot - 2)
     for slot in range(max(slots - 2, 0), slots):
@@ -207,7 +211,7 @@
     shared.wait()
 
 
-def exchange(owners, sections, lesser, greater, coupling):
+def exchange(owners, sections, lesser, greater, coulomb):
     local, count, _, width = lesser.shape
     slots = count // owners
     energies = local * owners
@@ -225,7 +229,7 @@
         in_specs=[anywhere] * 5,
         out_specs=[near] * (2 + sides),
         out_shape=[tile_shape] * (1 + sides)
-        + [jax.ShapeDtypeStruct(coupling.shape, coupling.dtype)],
+        + [jax.ShapeDtypeStruct(coulomb.shape[1:], coulomb.dtype)],
         scratch_shapes=[
             pltpu.VMEM((slots, 2, energies, 2, width), jnp.bfloat16),
             pltpu.VMEM((slots, energies, 2, width), jnp.bfloat16),
@@ -244,106 +248,111 @@
         compiler_params=pltpu.CompilerParams(
             collective_id=0, has_side_effects=True, vmem_limit_bytes=VMEM_LIMIT
         ),
-    )(lesser.reshape(split), greater.reshape(split), coupling, forward, inverse)
-
-
-def screen_kernel(count, terms, batch, *refs):
+    )(lesser.reshape(split), greater.reshape(split), coulomb, forward, inverse)
+
+
+def screen_setup(sections, coulomb_ref, other_ref, pattern_ref, right_ref, picked_ref, mask_ref):
+    terms, count, nb = mask_ref.shape
+    section = lax.axis_index("sec")
+    lower = other_ref[...].astype(jnp.float32).T
+    upper = coulomb_ref[1].astype(jnp.float32)
+    matrices = [coulomb_ref[0].astype(jnp.float32)]
+    if sections == 2:
+        sources = [section, 1 - section]
+        matrices.append(jnp.where(section == 0, upper, lower))
+    else:
+        sources = [
+            section,
+            lax.rem(section + sections - 1, sections),
+            lax.rem(section + 1, sections),
+        ]
+        matrices.append(jnp.where(section > 0, lower, 0.0))
+        matrices.append(jnp.where(section < sections - 1, upper, 0.0))
+    position = lax.broadcasted_iota(jnp.int32, (nb, TR * count), 0)
+    lane = lax.broadcasted_iota(jnp.int32, (count, nb), 1) // TC
+    first = lax.broadcasted_iota(jnp.int32, (count, count), 0)
+    second = lax.broadcasted_iota(jnp.int32, (count, count), 1)
+    across = nb // TC
+    for t in range(terms):
+        listed = pattern_ref[pl.ds(sources[t], 1), :]
+        row = jnp.concatenate([listed // across * TR + r for r in range(TR)], axis=1)
+        chosen = jnp.where(position == row, 1.0, 0.0).astype(jnp.bfloat16)
+        picked_ref[t] = dot32(matrices[t].astype(jnp.bfloat16), chosen).astype(jnp.bfloat16)
+        column = jnp.sum(
+            jnp.where(first == second, (listed % across).astype(jnp.float32), 0.0),
+            axis=1,
+            keepdims=True,
+        ).astype(jnp.int32)
+        mask_ref[t] = jnp.where(lane == column, 1.0, 0.0)
+        right_ref[t * nb : (t + 1) * nb] = matrices[t].T.astype(jnp.bfloat16)
+
+
+def screen_kernel(sections, terms, batch, *refs):
     tile_refs = refs[:terms]
-    matrix_ref, row_ref, col_ref, spread_ref, out_ref, picked_ref, mask_ref = refs[terms:]
-    nb = matrix_ref.shape[1]
+    coulomb_ref, other_ref, pattern_ref, out_ref = refs[terms : terms + 4]
+    right_ref, picked_ref, mask_ref, rows_ref = refs[terms + 4 :]
+    _, count, nb = mask_ref.shape
+    width = rows_ref.shape[-1]
 
     @pl.when(pl.program_id(0) == 0)
     def _():
-        for t in range(terms):
-            depth = row_ref.shape[2]
-            position = lax.broadcasted_iota(jnp.int32, (nb, depth), 0)
-            chosen = jnp.where(position == row_ref[t], 1.0, 0.0).astype(jnp.bfloat16)
-            picked_ref[t] = dot32(matrix_ref[t], chosen).astype(jnp.bfloat16)
-            lane = lax.broadcasted_iota(jnp.int32, (count, nb), 1) // TC
-            mask_ref[t] = jnp.where(lane == col_ref[t], 1.0, 0.0)
-
-    left = [[[] for _ in range(2)] for _ in range(batch)]
+        screen_setup(
+            sections, coulomb_ref, other_ref, pattern_ref, right_ref, picked_ref, mask_ref
+        )
+
+    lane = lax.broadcasted_iota(jnp.int32, (count, width), 1) % TC
+    joined = [[] for _ in range(batch * 2)]
     for t in range(terms):
-        width = spread_ref.shape[0]
-        rows = jnp.concatenate(
-            [tile_refs[t][b, :, c * width : (c + 1) * width] for b in range(batch) for c in range(2)],
-            axis=0,
-        )
-        wide = dot32(rows, spread_ref[...])
+        for b in range(batch):
+            rows_ref[t, b] = tile_refs[t][b].reshape(2 * count, width).astype(jnp.float32)
         mask = mask_ref[t]
         for b in range(batch):
             for c in range(2):
-                start = (2 * b + c) * count
-                pieces = [
-                    (wide[start : start + count, r * nb : (r + 1) * nb] * mask).astype(jnp.bfloat16)
-                    for r in range(TR)
-                ]
+                tile = rows_ref[t, b, pl.ds(c, count, stride=2), :]
+                pieces = []
+                for r in range(TR):
+                    spread = jnp.take_along_axis(
+                        tile, lane + r * TC, axis=1, mode="promise_in_bounds"
+                    )
+                    wide = jnp.concatenate([spread] * (nb // width), axis=1)
+                    pieces.append((wide * mask).astype(jnp.bfloat16))
                 stacked = jnp.concatenate(pieces, axis=0)
-                left[b][c].append(dot32(picked_ref[t], stacked).astype(jnp.bfloat16))
-    right = jnp.concatenate([matrix_ref[t] for t in range(terms)], axis=1)
-    for b in range(batch):
-        for c in range(2):
-            joined = jnp.concatenate(left[b][c], axis=1)
-            total = lax.dot_general(
-                joined, right, (((1,), (1,)), ((), ())), preferred_element_type=jnp.float32
-            )
-            out_ref[b, c] = total.astype(jnp.bfloat16)
-
-
-def screen(tiles, matrices, listed):
+                joined[2 * b + c].append(dot32(picked_ref[t], stacked).astype(jnp.bfloat16))
+    left = jnp.concatenate([jnp.concatenate(j, axis=1) for j in joined], axis=0)
+    total = dot32(left, right_ref[...]).astype(jnp.bfloat16)
+    out_ref[...] = total.reshape(batch, 2, nb, nb)
+
+
+def screen(sections, tiles, coulomb, other, pattern):
     terms = len(tiles)
-    energies, count, both = tiles[0].shape
-    nb = matrices.shape[1]
+    energies, owners, slots, _, width = tiles[0].shape
+    count = owners * slots
+    nb = coulomb.shape[1]
     batch = 2 if energies % 2 == 0 else 1
-    width = both // 2
-    tile_row = listed // (nb // TC)
-    tile_col = listed % (nb // TC)
-    offsets = jnp.arange(TR, dtype=jnp.int32)
-    row_index = (tile_row[:, None, :] * TR + offsets[None, :, None]).reshape(terms, 1, TR * count)
-    col_index = tile_col[:, :, None]
-    entry = np.arange(width)[:, None]
-    column = np.arange(TR * nb)[None, :]
-    spread = jnp.asarray(
-        (entry == column // nb * TC + column % TC).astype(np.float32).astype(jnp.bfloat16)
-    )
-    whole = lambda shape: pl.BlockSpec(shape, lambda i: (0,) * len(shape))
+    whole = lambda array: pl.BlockSpec(array.shape, lambda i: (0,) * array.ndim)
     return pl.pallas_call(
-        functools.partial(screen_kernel, count, terms, batch),
+        functools.partial(screen_kernel, sections, terms, batch),
         grid=(energies // batch,),
-        in_specs=[pl.BlockSpec((batch, count, both), lambda i: (i, 0, 0))] * terms
-        + [whole(matrices.shape), whole(row_index.shape), whole(col_index.shape), whole(spread.shape)],
+        in_specs=[pl.BlockSpec((batch, owners, slots, 2, width), lambda i: (i, 0, 0, 0, 0))] * terms
+        + [whole(coulomb), whole(other), whole(pattern)],
         out_specs=pl.BlockSpec((batch, 2, nb, nb), lambda i: (i, 0, 0, 0)),
         out_shape=jax.ShapeDtypeStruct((energies, 2, nb, nb), jnp.bfloat16),
         scratch_shapes=[
+            pltpu.VMEM((terms * nb, nb), jnp.bfloat16),
             pltpu.VMEM((terms, nb, TR * count), jnp.bfloat16),
             pltpu.VMEM((terms, count, nb), jnp.float32),
+            pltpu.VMEM((terms, batch, 2 * count, width), jnp.float32),
         ],
         compiler_params=pltpu.CompilerParams(vmem_limit_bytes=VMEM_LIMIT),
-    )(*tiles, matrices, row_index, col_index, spread)
+    )(*tiles, coulomb, other, pattern)
 
 
 def on_device(sections, owners, green_lesser, green_greater, coulomb, pattern):
     _, local, count, _, width = green_lesser.shape
-    section = lax.axis_index("sec")
     polar, *beside, other = exchange(
-        owners, sections, green_lesser[0], green_greater[0], coulomb[0, 1]
-    )
-    flat = lambda t: t.reshape(local, count, 2 * width)
-    matrices = [coulomb[0, 0]]
-    listed = [lax.dynamic_index_in_dim(pattern, section, 0, keepdims=False)]
-    if sections == 2:
-        matrices.append(jnp.where(section == 0, coulomb[0, 1], other.T))
-        listed.append(lax.dynamic_index_in_dim(pattern, 1 - section, 0, keepdims=False))
-    else:
-        before = lax.rem(section + sections - 1, sections)
-        after = lax.rem(section + 1, sections)
-        matrices.append(jnp.where(section > 0, other.T, 0))
-        matrices.append(jnp.where(section < sections - 1, coulomb[0, 1], 0))
-        listed.append(lax.dynamic_index_in_dim(pattern, before, 0, keepdims=False))
-        listed.append(lax.dynamic_index_in_dim(pattern, after, 0, keepdims=False))
-    screened = screen(
-        [flat(t) for t in (polar, *beside)], jnp.stack(matrices), jnp.stack(listed)
-    )
+        owners, sections, green_lesser[0], green_greater[0], coulomb[0]
+    )
+    screened = screen(sections, [polar, *beside], coulomb[0], other, pattern)
     return polar.reshape(1, local, count, 2, width), screened[None]
 
 

time: 76.1 us -> 65.6 us (0.86)
  local copies, waits for them, and re-layouts: 7.91 us -> 0.8 us
  other arithmetic: 2 us -> 0 us
  Pallas kernels: 65.2 us -> 64 us
    reshape x2 -> x0, local copies, waits for them, and re-layouts: 3.35 us -> none  [on_device(): flat = lambda t: t.reshape(local, count, 2 * width)]
    another operation x3 -> x0, local copies, waits for them, and re-layouts: 1.83 us -> none  [the longest x1 1.64 us: on_device(): jnp.stack(matrices)]
    pallas_call x1, Pallas kernels: 15 us -> 13.2 us  [screen(): pl.pallas_call(functools.partial(screen_kernel, sections, terms, batch),...]
    pallas_call x1 -> x0, local copies, waits for them, and re-layouts: 1 us -> none  [exchange(): pl.pallas_call(functools.partial(exchange_kernel, owners, sections, 1.0 /...]
    dynamic_slice x1 -> x0, local copies, waits for them, and re-layouts: 0.76 us -> none  [on_device(): listed = [lax.dynamic_index_in_dim(pattern, section, 0, keepdims=False)]]
where the time goes in v3:
time: 65.6 us; the launch traced here: 65.4 us
  Pallas kernels  64 us (98%)
  local copies, waits for them, and re-layouts  0.8 us (1%)
    pallas_call x1, Pallas kernels, exchange(): pl.pallas_call(functools.partial(exchange_kernel, owners, sections, 1.0 /...  50.8 us
    pallas_call x1, Pallas kernels, screen(): pl.pallas_call(functools.partial(screen_kernel, sections, terms, batch),...  13.2 us

profile of v3, /device:TPU:0, one launch (start us, length us, event | category | flops | bytes accessed | tf_op | source)
XLA Modules:
  0.0 65.4 jit_solution(5105434577837494271)
XLA Ops:
  0.6 50.8 %shard_map.77 = (bf16[16,16,4,2,128]{4,3,2,1,0:T(2,128)(2,1)}, bf16[16,16,4,2,128]{4,3,2,1,0:T(2,128)(2,1)}, bf16[256,256]{1,0:T(8,128)(2,1)}) custom-call(bf16[16,16,4,2,128]{4,3,2,1,0:T(2,128)(2,1)} %bitcast.9, bf16[16,16,4,2,128]{4,3,2,1,0:T(2,128)(2,1)} %bitcast.10, bf16[2,256,256]{2,1,0:T(8,128)(2,1)} %bitcast.7, ...), custom_call_target="tpu_custom_call" | custom-call | tf_op jit(solution)/shard_map/pallas_call | solution.py:225
  51.4 0.0 copy-start
  51.4 13.2 %shard_map.78 = bf16[16,2,256,256]{3,2,1,0:T(8,128)(2,1)} custom-call(bf16[16,16,4,2,128]{4,3,2,1,0:T(2,128)(2,1)} %get-tuple-element.5.refs_0_, bf16[16,16,4,2,128]{4,3,2,1,0:T(2,128)(2,1)} %get-tuple-element.6.refs_1_, bf16[2,256,256]{2,1,0:T(8,128)(2,1)} %bitcast.8, bf16[256,256]{1,0:T(8,128)(2,1)} %get-tuple-element.7.refs_3_, s32[2,64]{1,0:T(2,128)} %refs_4_.1), custom_call_target="tpu_custom_call" | custom-call | tf_op jit(solution)/shard_map/pallas_call | solution.py:333
  64.6 0.0 copy-done
  64.6 0.8 %copy.9 = bf16[1,16,64,2,128]{4,3,2,1,0:T(2,128)(2,1)} copy(bf16[1,16,64,2,128]{4,3,2,1,0:T(2,128)(2,1)S(1)} %bitcast.6) | data formatting | bytes 1048576
Async XLA Ops:
  51.4 13.2 %copy-start = (bf16[16,16,4,2,128]{4,3,2,1,0:T(2,128)(2,1)S(1)}, bf16[16,16,4,2,128]{4,3,2,1,0:T(2,128)(2,1)}, u32[]{:S(2)}) copy-start(bf16[16,16,4,2,128]{4,3,2,1,0:T(2,128)(2,1)} %get-tuple-element.5.refs_0_) | copy-start | bytes 1572868

commit v4 on v3

--- a/solution.py
+++ b/solution.py
@@ -283,7 +283,7 @@
             axis=1,
             keepdims=True,
         ).astype(jnp.int32)
-        mask_ref[t] = jnp.where(lane == column, 1.0, 0.0)
+        mask_ref[t] = jnp.where(lane == column, 1.0, 0.0).astype(jnp.bfloat16)
         right_ref[t * nb : (t + 1) * nb] = matrices[t].T.astype(jnp.bfloat16)
 
 
@@ -314,8 +314,9 @@
                     spread = jnp.take_along_axis(
                         tile, lane + r * TC, axis=1, mode="promise_in_bounds"
                     )
+                    spread = spread.astype(jnp.bfloat16)
                     wide = jnp.concatenate([spread] * (nb // width), axis=1)
-                    pieces.append((wide * mask).astype(jnp.bfloat16))
+                    pieces.append(wide * mask)
                 stacked = jnp.concatenate(pieces, axis=0)
                 joined[2 * b + c].append(dot32(picked_ref[t], stacked).astype(jnp.bfloat16))
     left = jnp.concatenate([jnp.concatenate(j, axis=1) for j in joined], axis=0)
@@ -328,7 +329,7 @@
     energies, owners, slots, _, width = tiles[0].shape
     count = owners * slots
     nb = coulomb.shape[1]
-    batch = 2 if energies % 2 == 0 else 1
+    batch = next(n for n in (4, 2, 1) if energies % n == 0)
     whole = lambda array: pl.BlockSpec(array.shape, lambda i: (0,) * array.ndim)
     return pl.pallas_call(
         functools.partial(screen_kernel, sections, terms, batch),
@@ -340,7 +341,7 @@
         scratch_shapes=[
             pltpu.VMEM((terms * nb, nb), jnp.bfloat16),
             pltpu.VMEM((terms, nb, TR * count), jnp.bfloat16),
-            pltpu.VMEM((terms, count, nb), jnp.float32),
+            pltpu.VMEM((terms, count, nb), jnp.bfloat16),
             pltpu.VMEM((terms, batch, 2 * count, width), jnp.float32),
         ],
         compiler_params=pltpu.CompilerParams(vmem_limit_bytes=VMEM_LIMIT),

time: 65.6 us -> 63 us (0.960)
  Pallas kernels: 64 us -> 61.4 us
    pallas_call x1, Pallas kernels: 13.2 us -> 10.6 us  [screen(): pl.pallas_call(functools.partial(screen_kernel, sections, terms, batch),...]
where the time goes in v4:
time: 63 us; the launch traced here: 62.9 us
  Pallas kernels  61.4 us (97%)
  local copies, waits for them, and re-layouts  0.8 us (1%)
  between operations  0.65 us (1%)
    pallas_call x1, Pallas kernels, exchange(): pl.pallas_call(functools.partial(exchange_kernel, owners, sections, 1.0 /...  50.8 us
    pallas_call x1, Pallas kernels, screen(): pl.pallas_call(functools.partial(screen_kernel, sections, terms, batch),...  10.6 us

profile of v4, /device:TPU:0, one launch (start us, length us, event | category | flops | bytes accessed | tf_op | source)
XLA Modules:
  0.0 62.9 jit_solution(17751645643828488318)
XLA Ops:
  0.6 50.8 %shard_map.77 = (bf16[16,16,4,2,128]{4,3,2,1,0:T(2,128)(2,1)}, bf16[16,16,4,2,128]{4,3,2,1,0:T(2,128)(2,1)}, bf16[256,256]{1,0:T(8,128)(2,1)}) custom-call(bf16[16,16,4,2,128]{4,3,2,1,0:T(2,128)(2,1)} %bitcast.9, bf16[16,16,4,2,128]{4,3,2,1,0:T(2,128)(2,1)} %bitcast.10, bf16[2,256,256]{2,1,0:T(8,128)(2,1)} %bitcast.7, ...), custom_call_target="tpu_custom_call" | custom-call | tf_op jit(solution)/shard_map/pallas_call | solution.py:225
  51.4 0.0 copy-start
  51.4 10.6 %shard_map.78 = bf16[16,2,256,256]{3,2,1,0:T(8,128)(2,1)} custom-call(bf16[16,16,4,2,128]{4,3,2,1,0:T(2,128)(2,1)} %get-tuple-element.5.refs_0_, bf16[16,16,4,2,128]{4,3,2,1,0:T(2,128)(2,1)} %get-tuple-element.6.refs_1_, bf16[2,256,256]{2,1,0:T(8,128)(2,1)} %bitcast.8, bf16[256,256]{1,0:T(8,128)(2,1)} %get-tuple-element.7.refs_3_, s32[2,64]{1,0:T(2,128)} %refs_4_.1), custom_call_target="tpu_custom_call" | custom-call | tf_op jit(solution)/shard_map/pallas_call | solution.py:334
  62.1 0.0 copy-done
  62.1 0.8 %copy.9 = bf16[1,16,64,2,128]{4,3,2,1,0:T(2,128)(2,1)} copy(bf16[1,16,64,2,128]{4,3,2,1,0:T(2,128)(2,1)S(1)} %bitcast.6) | data formatting | bytes 1048576
Async XLA Ops:
  51.4 10.6 %copy-start = (bf16[16,16,4,2,128]{4,3,2,1,0:T(2,128)(2,1)S(1)}, bf16[16,16,4,2,128]{4,3,2,1,0:T(2,128)(2,1)}, u32[]{:S(2)}) copy-start(bf16[16,16,4,2,128]{4,3,2,1,0:T(2,128)(2,1)} %get-tuple-element.5.refs_0_) | copy-start | bytes 1572868

commit v5 on v4

--- a/solution.py
+++ b/solution.py
@@ -117,8 +117,7 @@
     pl.semaphore_wait(barrier, owners - 1 + sides)
 
     def peer_at(turn):
-        away = (turn + 1) // 2 * (2 * (turn % 2) - 1)
-        return lax.rem(me + owners // 2 + away, owners)
+        return lax.rem(me + 1 + turn, owners)
 
     mine = pl.ds(me * local, local)
     for slot in range(slots):
@@ -329,7 +328,7 @@
     energies, owners, slots, _, width = tiles[0].shape
     count = owners * slots
     nb = coulomb.shape[1]
-    batch = next(n for n in (4, 2, 1) if energies % n == 0)
+    batch = next(n for n in (8, 4, 2, 1) if energies % n == 0)
     whole = lambda array: pl.BlockSpec(array.shape, lambda i: (0,) * array.ndim)
     return pl.pallas_call(
         functools.partial(screen_kernel, sections, terms, batch),

time: 63 us -> 62.3 us (0.989)
  Pallas kernels: 61.4 us -> 60.7 us
where the time goes in v5:
time: 62.3 us; the launch traced here: 62.1 us
  Pallas kernels  60.7 us (97%)
  local copies, waits for them, and re-layouts  0.8 us (1%)
  between operations  0.65 us (1%)
    pallas_call x1, Pallas kernels, exchange(): pl.pallas_call(functools.partial(exchange_kernel, owners, sections, 1.0 /...  50.3 us
    pallas_call x1, Pallas kernels, screen(): pl.pallas_call(functools.partial(screen_kernel, sections, terms, batch),...  10.4 us

profile of v5, /device:TPU:0, one launch (start us, length us, event | category | flops | bytes accessed | tf_op | source)
XLA Modules:
  0.0 62.1 jit_solution(542567075840404639)
XLA Ops:
  0.6 50.3 %shard_map.77 = (bf16[16,16,4,2,128]{4,3,2,1,0:T(2,128)(2,1)}, bf16[16,16,4,2,128]{4,3,2,1,0:T(2,128)(2,1)}, bf16[256,256]{1,0:T(8,128)(2,1)}) custom-call(bf16[16,16,4,2,128]{4,3,2,1,0:T(2,128)(2,1)} %bitcast.9, bf16[16,16,4,2,128]{4,3,2,1,0:T(2,128)(2,1)} %bitcast.10, bf16[2,256,256]{2,1,0:T(8,128)(2,1)} %bitcast.7, ...), custom_call_target="tpu_custom_call" | custom-call | tf_op jit(solution)/shard_map/pallas_call | solution.py:224
  50.9 0.0 copy-start
  50.9 10.4 %shard_map.78 = bf16[16,2,256,256]{3,2,1,0:T(8,128)(2,1)} custom-call(bf16[16,16,4,2,128]{4,3,2,1,0:T(2,128)(2,1)} %get-tuple-element.5.refs_0_, bf16[16,16,4,2,128]{4,3,2,1,0:T(2,128)(2,1)} %get-tuple-element.6.refs_1_, bf16[2,256,256]{2,1,0:T(8,128)(2,1)} %bitcast.8, bf16[256,256]{1,0:T(8,128)(2,1)} %get-tuple-element.7.refs_3_, s32[2,64]{1,0:T(2,128)} %refs_4_.1), custom_call_target="tpu_custom_call" | custom-call | tf_op jit(solution)/shard_map/pallas_call | solution.py:333
  61.3 0.0 copy-done
  61.3 0.8 %copy.9 = bf16[1,16,64,2,128]{4,3,2,1,0:T(2,128)(2,1)} copy(bf16[1,16,64,2,128]{4,3,2,1,0:T(2,128)(2,1)S(1)} %bitcast.6) | data formatting | bytes 1048576
Async XLA Ops:
  50.9 10.4 %copy-start = (bf16[16,16,4,2,128]{4,3,2,1,0:T(2,128)(2,1)S(1)}, bf16[16,16,4,2,128]{4,3,2,1,0:T(2,128)(2,1)}, u32[]{:S(2)}) copy-start(bf16[16,16,4,2,128]{4,3,2,1,0:T(2,128)(2,1)} %get-tuple-element.5.refs_0_) | copy-start | bytes 1572868
